TPU v7x, 32 devices: a whole 2x2x4 slice. The times are simulated.
32 devices in a mesh: group: 2 (over y), sta: 4 (over z), win: 2 (over x), freq: 2 (over core).
Axes of the slice: x: 2, y: 2, z: 4, core: 2. Of those that a mesh axis runs over, the one named last changes fastest.
Arguments:
- records: float32 [1024, 4, 3600], P(('group', 'sta'), 'win', 'freq'), parts along dimension 0, may hold values from -6 to 6
- valid_counts: int32 [8], P(('group', 'sta')), parts along dimension 0, may hold values from 64 to 128, as said below
- pair_blocks: int32 [8, 2], P('group'), parts along dimension 0, may hold values from 0 to 3, as said below
Outputs:
- pair_spectra: bfloat16 [8, 2, 256, 2, 128, 128], P(('group', 'sta'), 'freq', 'win'), parts along dimension 0
There are 2 independent parts, one for each index of `group`. A program takes and returns all parts, laid end to end along the dimension named above; each array names one. Nothing has to cross between parts.
Inputs may be any that keep to these rules, and one draw needn't show every extreme that they name: The stations of block i at positions below valid_counts[i] are live, the others are masked out. `pair_blocks`: slot k belongs to index k // 1 of sta and names two station blocks.
All inputs are finite; a program needn't handle non-finite values.
Results may differ from a plain program's by a relative error of at most 0.001.
Values may be sent and summed in bfloat16 or wider, within the bound.
A program may use at most 64 MiB of HBM per device.

v0:
```python
import math
import jax
import jax.numpy as jnp
from jax import lax
from jax.sharding import PartitionSpec as P

SAMPLES = 3600
BINS = 512
HALF_WIDTH = 10
TWO_PI = 2.0 * math.pi
AMP_FLOOR = 0.1
PRECISE = lax.Precision.HIGHEST


def padded_2(value, sides, width):
    for axis, dim in sides:
        peers, length = (lax.axis_size(axis), value.shape[dim])
        up = [(i, (i + 1) % peers) for i in range(peers - 1)]
        down = [(j, i) for i, j in up]
        last = lax.slice_in_dim(value, length - width, length, axis=dim)
        first = lax.slice_in_dim(value, 0, width, axis=dim)
        before = lax.ppermute(last, axis, up)
        after = lax.ppermute(first, axis, down)
        value = jnp.concatenate([before, value, after], axis=dim)
    return value


def taper_of(sample_index, length_all):
    edge_len = length_all // 20
    position = jnp.minimum(sample_index, length_all - 1 - sample_index)
    ramped = 0.5 * (1.0 - jnp.cos(math.pi * (position.astype(jnp.float32) + 0.5) / edge_len))
    return jnp.where(position < edge_len, ramped, 1.0)


def dft_tables(bin_start, amount, sample_count, length_all):
    bin_index = bin_start + 1 + lax.broadcasted_iota(jnp.int32, (amount, sample_count), 0)
    sample_index = lax.broadcasted_iota(jnp.int32, (amount, sample_count), 1)
    angles = (bin_index * sample_index % length_all).astype(jnp.float32) * (TWO_PI / length_all)
    weight = taper_of(sample_index, length_all) / math.sqrt(length_all)
    return (jnp.cos(angles) * weight, -jnp.sin(angles) * weight)


def cross_pair(left_block, right_block):
    left_real = left_block[:, :, 0]
    left_imag = left_block[:, :, 1]
    stacked = jnp.stack(
        (jnp.stack((left_real, left_imag), 2), jnp.stack((left_imag, -left_real), 2)), 1
    )
    factor = 1.0 / math.sqrt(left_block.shape[1])
    return jnp.einsum("fpwqa,fwqb->fpab", stacked, right_block, precision=PRECISE) * factor


def local(records, valid_counts, pair_blocks):
    block_size = records.shape[0]
    band_bins = BINS // lax.axis_size("freq")
    first_bin = lax.axis_index("freq") * band_bins
    portion = lax.all_gather(records, "freq", axis=2, tiled=True)
    cos_table, sin_table = dft_tables(first_bin, band_bins, portion.shape[2], SAMPLES)
    real_part = jnp.einsum("kn,swn->kws", cos_table, portion, precision=PRECISE)
    imag_part = jnp.einsum("kn,swn->kws", sin_table, portion, precision=PRECISE)
    spectrum = jnp.stack((real_part, imag_part), 2)
    live_mask = (lax.broadcasted_iota(jnp.int32, (block_size,), 0) < valid_counts[0]).astype(
        jnp.float32
    )
    spectrum = spectrum * live_mask
    magnitude = jnp.sqrt(
        spectrum[:, :, 0] * spectrum[:, :, 0] + spectrum[:, :, 1] * spectrum[:, :, 1]
    )
    padded = padded_2(magnitude, (("freq", 0),), HALF_WIDTH)
    row_index = lax.broadcasted_iota(jnp.int32, (band_bins, band_bins + 2 * HALF_WIDTH), 0)
    col_index = lax.broadcasted_iota(jnp.int32, (band_bins, band_bins + 2 * HALF_WIDTH), 1)
    box_matrix = ((col_index - row_index >= 0) & (col_index - row_index <= 2 * HALF_WIDTH)).astype(
        jnp.float32
    )
    summed = jnp.einsum("ij,jws->iws", box_matrix, padded, precision=PRECISE)
    global_bin = first_bin + lax.broadcasted_iota(jnp.int32, (band_bins,), 0)
    counted = (
        jnp.minimum(global_bin + HALF_WIDTH, BINS - 1) - jnp.maximum(global_bin - HALF_WIDTH, 0) + 1
    ).astype(jnp.float32)
    smooth = summed / counted[:, None, None]
    whitened = spectrum / jnp.maximum(smooth, AMP_FLOOR)[:, :, None, :]
    sta_count = lax.axis_size("sta")
    slots = pair_blocks.shape[0] // sta_count
    my_slots = lax.dynamic_slice_in_dim(pair_blocks, lax.axis_index("sta") * slots, slots, 0)
    held_block = lax.all_to_all(whitened, "win", split_axis=0, concat_axis=1, tiled=True)
    blank_pair = jnp.zeros((slots,) + held_block.shape, jnp.float32)
    carried = (blank_pair, blank_pair)
    portion = lax.all_gather(held_block[None], "sta", axis=0, tiled=True)
    amount = portion.shape[0]
    chosen = []
    for column in range(2):
        wanted = my_slots[:, column]
        inside = (wanted >= 0) & (wanted < amount)
        fetched = jnp.take(portion, jnp.clip(wanted, 0, amount - 1), axis=0)
        chosen.append(jnp.where(inside[:, None, None, None, None], fetched, carried[column]))
    left_blocks = chosen[0]
    right_blocks = chosen[1]
    mixed = jax.vmap(cross_pair)(left_blocks, right_blocks).astype(jnp.bfloat16)
    return mixed[:, None]


def solution(mesh):
    in_specs = (P(("group", "sta"), "win", "freq"), P(("group", "sta")), P("group", None))
    out_specs = P(("group", "sta"), "freq", "win", None, None, None)
    return jax.shard_map(local, mesh=mesh, in_specs=in_specs, out_specs=out_specs, check_vma=False)
```

profile of v0, /device:TPU:0, one launch (start us, length us, event | category | flops | bytes accessed | tf_op | source)
XLA Modules:
  0.0 175.7 jit_solution(15182454830260234039)
XLA Ops:
  6.5 0.0 copy-start
  6.5 0.0 all-gather.3.cloned.1.call-start
  6.5 0.7 all-gather.3.cloned.1.call-update
  7.3 0.0 all-gather.5.cloned.1.call-start
  8.0 0.1 subtract_multiply_fusion
  8.1 16.5 %all-gather.3.cloned.1.call-done = f32[128,2,3600]{0,2,1:T(8,128)} async-done(((f32[128,2,1800]{0,2,1:T(8,128)}), f32[128,2,3600]{0,2,1:T(8,128)}) %all-gather.3.cloned.1.call-update) | async-done | bytes 3686416 | tf_op jit(solution)/shard_map/all_gather | solution.py:57
  24.6 0.0 copy-start.1
  24.6 25.0 %fusion.37 = f32[256,2,1,128]{3,0,1,2:T(8,128)S(1)} fusion(f32[128,2,3600]{0,2,1:T(8,128)} %all-gather.3.cloned.1.call-done, f32[3600]{0:T(1024)S(1)} %subtract_multiply_fusion, s32[256]{0:T(256)S(1)} %iota_add_fusion, pred[3600]{0:T(1024)(128)(4,1)S(1)} %fusion.65), kind=kOutput, calls=%fused_computation.35 | convolution fusion | flops 2843136000 | bytes 3967568 | tf_op jit(solution)/shard_map/kn,swn->kws/dot_general | solution.py:60
  49.6 0.0 copy-done.1
  49.6 21.3 %fusion.34 = f32[256,2,1,128]{3,0,1,2:T(8,128)S(1)} fusion(f32[128,2,3600]{0,2,1:T(8,128)S(1)} %copy-done.1, f32[3600]{0:T(1024)S(1)} %subtract_multiply_fusion, s32[256]{0:T(256)S(1)} %iota_add_fusion, pred[3600]{0:T(1024)(128)(4,1)S(1)} %fusion.65), kind=kOutput, calls=%fused_computation.34 | convolution fusion | flops 2842214400 | bytes 3967568 | tf_op jit(solution)/shard_map/kn,swn->kws/dot_general | solution.py:59
  70.9 0.1 fusion.58
  71.1 2.1 %collective-permute-start = (f32[10,2,128]{2,0,1:T(8,128)S(1)}, f32[10,2,128]{2,0,1:T(8,128)S(1)}, u32[]{:S(2)}, u32[]{:S(2)}) collective-permute-start(f32[10,2,128]{2,0,1:T(8,128)S(1)} %get-tuple-element.21), channel_id=1, source_target_pairs={{0,1},{2,3},{4,5},{6,7},{8,9},{10,11},{12,13},{14,15},{16,17},{18,... | collective-permute-start | bytes 30728 | tf_op jit(solution)/shard_map/ppermute | solution.py:22
  73.2 1.3 collective-permute-start.1
  74.5 0.1 fusion.86
  74.6 0.0 collective-permute-done
  74.6 1.7 collective-permute-done.1
  76.3 0.5 fusion.40
  76.8 0.1 broadcast_divide_fusion
  76.8 0.4 copy.6
  77.3 11.3 %all_to_all.15 = f32[256,2,2,128]{3,1,2,0:T(2,128)S(1)} all-to-all(f32[256,2,2,128]{3,1,2,0:T(2,128)S(1)} %copy.6), channel_id=1, replica_groups=mesh['group'=2,'sta'=4,'win'=2,'freq'=2] {'win'}, dimensions={0} | all-to-all | bytes 1048576 | tf_op jit(solution)/shard_map/all_to_all | solution.py:85
  88.5 0.8 copy.7
  89.3 0.0 all-gather.5.cloned.1.call-update
  89.4 0.0 copy-done
  89.4 0.1 constant_dynamic-slice_fusion.2
  89.4 0.5 fusion.82
  93.5 42.0 %all-gather.5.cloned.1.call-done = f32[4,128,4,2,128]{4,1,3,2,0:T(8,128)} async-done(((f32[1,128,4,2,128]{4,1,3,2,0:T(8,128)}), f32[4,128,4,2,128]{4,1,3,2,0:T(8,128)}) %all-gather.5.cloned.1.call-update) | async-done | bytes 2097168 | tf_op jit(solution)/shard_map/all_gather | solution.py:88
  135.6 1.3 constant_dynamic-slice_fusion
  136.8 0.5 fusion.85
  137.3 0.5 fusion.45
  137.8 0.1 fusion.81
  137.9 0.1 maximum_bitcast_fusion.1
  138.0 30.8 %fusion.1 = bf16[1,1,128,2,128,128]{5,4,3,2,1,0:T(8,128)(2,1)} fusion(f32[1,128,4,2,128]{4,1,3,2,0:T(8,128)S(1)} %get-tuple-element.17, pred[]{:T(512)} %bitcast.23, pred[]{:T(512)} %bitcast.21, f32[1,128,1,4,2,128]{5,3,4,1,2,0:T(4,128)S(1)} %maximum_bitcast_fusion.1, f32[1,128,1,4,2,128]{5,3,4,1,2,0:T(4,128)S(1)} %fusion.85), kind=kOutput, calls=%fused_computation.3 | convolution fusion | flops 411566080 | bytes 9961474 | tf_op jit(solution)/shard_map/vmap(fpwqa,fwqb->fpab)/dot_general | solution.py:50
  (6 shorter events, 0.1 us)
Async XLA Ops:
  6.5 82.8 %copy-start = (s32[4,2]{0,1:T(2,128)S(1)}, s32[4,2]{0,1:T(2,128)}, u32[]{:S(2)}) copy-start(s32[4,2]{0,1:T(2,128)} %param.7) | copy-start | bytes 100
  6.5 18.0 %all-gather.3.cloned.1.call-start = ((), (), s32[]{:S(2)}) async-start(), calls=%async_computation.1 | async-start | bytes 5529600 | tf_op jit(solution)/shard_map/all_gather | solution.py:57
  7.3 128.3 %all-gather.5.cloned.1.call-start = ((), (), s32[]{:S(2)}) async-start(), calls=%async_computation.2 | async-start | bytes 2621440 | tf_op jit(solution)/shard_map/all_gather | solution.py:88
  24.6 25.0 %copy-start.1 = (f32[128,2,3600]{0,2,1:T(8,128)S(1)}, f32[128,2,3600]{0,2,1:T(8,128)}, u32[]{:S(2)}) copy-start(f32[128,2,3600]{0,2,1:T(8,128)} %all-gather.3.cloned.1.call-done) | copy-start | bytes 11059204
  71.1 3.5 %collective-permute-start = (f32[10,2,128]{2,0,1:T(8,128)S(1)}, f32[10,2,128]{2,0,1:T(8,128)S(1)}, u32[]{:S(2)}, u32[]{:S(2)}) collective-permute-start(f32[10,2,128]{2,0,1:T(8,128)S(1)} %get-tuple-element.21), channel_id=1, source_target_pairs={{0,1},{2,3},{4,5},{6,7},{8,9},{10,11},{12,13},{14,15},{16,17},{18,... | collective-permute-start | bytes 30728 | tf_op jit(solution)/shard_map/ppermute | solution.py:22
  73.2 3.1 %collective-permute-start.1 = (f32[10,2,128]{2,0,1:T(8,128)S(1)}, f32[10,2,128]{2,0,1:T(8,128)S(1)}, u32[]{:S(2)}, u32[]{:S(2)}) collective-permute-start(f32[10,2,128]{2,0,1:T(8,128)S(1)} %get-tuple-element.22), channel_id=1, source_target_pairs={{1,0},{3,2},{5,4},{7,6},{9,8},{11,10},{13,12},{15,14},{17,16},{19,... | collective-permute-start | bytes 30728 | tf_op jit(solution)/shard_map/ppermute | solution.py:23
Sparse Core Ops, SparseCore 0:
  8.9 15.6 all-gather.2
  89.5 46.0 all-gather.4
where the time goes:
time: 176 us
  matrix products  77.6 us (44%)
  waiting for transfers between devices  60.9 us (35%)
  between operations  17.8 us (10%)
  blocking collectives  11.3 us (6%)
  starting transfers between devices  3.45 us (2%)
  local copies, waits for them, and re-layouts  3.12 us (2%)
    all_gather x1, waiting for transfers between devices, local(): portion = lax.all_gather(held_block[None], 'sta', axis=0, tiled=True)  42 us
    dot_general x1, matrix products, cross_pair(): jnp.einsum('fpwqa,fwqb->fpab', stacked, right_block, precision=PRECISE)  30.8 us
    dot_general x1, matrix products, local(): imag_part = jnp.einsum('kn,swn->kws', sin_table, portion, precision=PRECISE)  25 us
    dot_general x1, matrix products, local(): real_part = jnp.einsum('kn,swn->kws', cos_table, portion, precision=PRECISE)  21.3 us
    all_gather x1, waiting for transfers between devices, local(): portion = lax.all_gather(records, 'freq', axis=2, tiled=True)  16.5 us
    all_to_all x1, blocking collectives, local(): lax.all_to_all(whitened, 'win', split_axis=0, concat_axis=1, tiled=True)  11.3 us
  transfers between devices with their start and end apart: 4, of which 3 were waited for; matrix products, arithmetic and copies ran while one was open for 0% of the time, Pallas kernels for 0%

commit v1 on v0

--- a/solution.py
+++ b/solution.py
@@ -10,6 +10,25 @@
 TWO_PI = 2.0 * math.pi
 AMP_FLOOR = 0.1
 PRECISE = lax.Precision.HIGHEST
+
+
+def gather_around(x, axis, dim):
+    peers, here, span = (lax.axis_size(axis), lax.axis_index(axis), x.shape[dim])
+    ahead = [(i, (i + 1) % peers) for i in range(peers)]
+    left = [(i, (i - 1) % peers) for i in range(peers)]
+    out = jnp.zeros((*x.shape[:dim], peers * span, *x.shape[dim + 1 :]), x.dtype)
+    out = lax.dynamic_update_slice_in_dim(out, x, here * span, axis=dim)
+    from_left = from_right = x
+    halfway = peers // 2
+    for lap in range(1, halfway + 1):
+        from_left = lax.ppermute(from_left, axis, ahead)
+        out = lax.dynamic_update_slice_in_dim(out, from_left, (here - lap) % peers * span, axis=dim)
+        if lap < peers - halfway:
+            from_right = lax.ppermute(from_right, axis, left)
+            out = lax.dynamic_update_slice_in_dim(
+                out, from_right, (here + lap) % peers * span, axis=dim
+            )
+    return out
 
 
 def padded_2(value, sides, width):
@@ -85,7 +104,7 @@
     held_block = lax.all_to_all(whitened, "win", split_axis=0, concat_axis=1, tiled=True)
     blank_pair = jnp.zeros((slots,) + held_block.shape, jnp.float32)
     carried = (blank_pair, blank_pair)
-    portion = lax.all_gather(held_block[None], "sta", axis=0, tiled=True)
+    portion = gather_around(held_block[None], "sta", 0)
     amount = portion.shape[0]
     chosen = []
     for column in range(2):

time: 176 us -> 165 us (0.938)
  waiting for transfers between devices: 60.9 us -> 47.3 us
  starting transfers between devices: 3.45 us -> 7.29 us
    all_gather x1 -> x0, waiting for transfers between devices: 42 us -> none  [local(): portion = lax.all_gather(held_block[None], 'sta', axis=0, tiled=True)]
    ppermute x0 -> x3, waiting for transfers between devices: none -> 28.4 us  [the longest x2 23 us: gather_around(): from_left = lax.ppermute(from_left, axis, ahead)]
    ppermute x0 -> x3, starting transfers between devices: none -> 3.88 us  [the longest x1 2.18 us: gather_around(): from_right = lax.ppermute(from_right, axis, left)]
  transfers between devices with their start and end apart: 4 -> 6, of which waited for: 3 -> 5; matrix products, arithmetic and copies ran while one was open for 0% -> 1% of each run, Pallas kernels for 0% -> 0%
where the time goes in v1:
time: 165 us; the launch traced here: 164 us
  matrix products  77.8 us (47%)
  waiting for transfers between devices  47.3 us (29%)
  between operations  18.1 us (11%)
  blocking collectives  11.2 us (7%)
  starting transfers between devices  7.29 us (4%)
  local copies, waits for them, and re-layouts  1.78 us (1%)
    dot_general x1, matrix products, cross_pair(): jnp.einsum('fpwqa,fwqb->fpab', stacked, right_block, precision=PRECISE)  31 us
    dot_general x1, matrix products, local(): imag_part = jnp.einsum('kn,swn->kws', sin_table, portion, precision=PRECISE)  25 us
    ppermute x2, waiting for transfers between devices, gather_around(): from_left = lax.ppermute(from_left, axis, ahead)  23 us
    dot_general x1, matrix products, local(): real_part = jnp.einsum('kn,swn->kws', cos_table, portion, precision=PRECISE)  21.3 us
    all_gather x1, waiting for transfers between devices, local(): portion = lax.all_gather(records, 'freq', axis=2, tiled=True)  16.5 us
    all_to_all x1, blocking collectives, local(): lax.all_to_all(whitened, 'win', split_axis=0, concat_axis=1, tiled=True)  11.2 us
    ppermute x1, waiting for transfers between devices, gather_around(): from_right = lax.ppermute(from_right, axis, left)  5.43 us
  transfers between devices with their start and end apart: 6, of which 5 were waited for; matrix products, arithmetic and copies ran while one was open for 1% of the time, Pallas kernels for 0%

profile of v1, /device:TPU:0, one launch (start us, length us, event | category | flops | bytes accessed | tf_op | source)
XLA Modules:
  0.0 164.4 jit_solution(17804319026015250266)
XLA Ops:
  6.5 0.7 all-gather.2.cloned.1.call-update
  8.0 0.1 subtract_multiply_fusion
  8.0 16.5 %all-gather.2.cloned.1.call-done = f32[128,2,3600]{0,2,1:T(8,128)} async-done(((f32[128,2,1800]{0,2,1:T(8,128)}), f32[128,2,3600]{0,2,1:T(8,128)}) %all-gather.2.cloned.1.call-update) | async-done | bytes 3686416 | tf_op jit(solution)/shard_map/all_gather | solution.py:76
  24.6 25.0 %fusion.37 = f32[256,2,1,128]{3,0,1,2:T(8,128)S(1)} fusion(f32[128,2,3600]{0,2,1:T(8,128)} %all-gather.2.cloned.1.call-done, f32[3600]{0:T(1024)S(1)} %subtract_multiply_fusion, s32[256]{0:T(256)S(1)} %iota_add_fusion, pred[3600]{0:T(1024)(128)(4,1)S(1)} %fusion.63), kind=kOutput, calls=%fused_computation.35 | convolution fusion | flops 2843136000 | bytes 3967568 | tf_op jit(solution)/shard_map/kn,swn->kws/dot_general | solution.py:79
  49.6 21.3 %fusion.34 = f32[256,2,1,128]{3,0,1,2:T(8,128)S(1)} fusion(f32[128,2,3600]{0,2,1:T(8,128)S(1)} %copy-done.1, f32[3600]{0:T(1024)S(1)} %subtract_multiply_fusion, s32[256]{0:T(256)S(1)} %iota_add_fusion, pred[3600]{0:T(1024)(128)(4,1)S(1)} %fusion.63), kind=kOutput, calls=%fused_computation.34 | convolution fusion | flops 2842214400 | bytes 3967568 | tf_op jit(solution)/shard_map/kn,swn->kws/dot_general | solution.py:78
  71.0 0.1 fusion.56
  71.1 2.1 %collective-permute-start = (f32[10,2,128]{2,0,1:T(8,128)S(1)}, f32[10,2,128]{2,0,1:T(8,128)S(1)}, u32[]{:S(2)}, u32[]{:S(2)}) collective-permute-start(f32[10,2,128]{2,0,1:T(8,128)S(1)} %get-tuple-element.19), channel_id=1, source_target_pairs={{0,1},{2,3},{4,5},{6,7},{8,9},{10,11},{12,13},{14,15},{16,17},{18,... | collective-permute-start | bytes 30728 | tf_op jit(solution)/shard_map/ppermute | solution.py:41
  73.2 1.3 collective-permute-start.1
  74.5 0.1 fusion.85
  74.6 1.7 %collective-permute-done.1 = f32[10,2,128]{2,0,1:T(8,128)S(1)} collective-permute-done((f32[10,2,128]{2,0,1:T(8,128)S(1)}, f32[10,2,128]{2,0,1:T(8,128)S(1)}, u32[]{:S(2)}, u32[]{:S(2)}) %collective-permute-start.1) | collective-permute-done | bytes 10272 | tf_op jit(solution)/shard_map/ppermute | solution.py:42
  76.3 0.5 fusion.40
  76.8 0.1 broadcast_divide_fusion
  76.8 0.4 copy.6
  77.3 11.2 %all_to_all.15 = f32[256,2,2,128]{3,1,2,0:T(2,128)S(1)} all-to-all(f32[256,2,2,128]{3,1,2,0:T(2,128)S(1)} %copy.6), channel_id=1, replica_groups=mesh['group'=2,'sta'=4,'win'=2,'freq'=2] {'win'}, dimensions={0} | all-to-all | bytes 1048576 | tf_op jit(solution)/shard_map/all_to_all | solution.py:104
  88.4 0.2 copy.7
  88.6 1.7 %collective-permute-start.2 = (f32[1,128,4,2,128]{4,2,3,1,0:T(4,128)S(1)}, f32[1,128,4,2,128]{4,2,3,1,0:T(4,128)S(1)}, u32[]{:S(2)}, u32[]{:S(2)}) collective-permute-start(f32[1,128,4,2,128]{4,2,3,1,0:T(4,128)S(1)} %bitcast.66), channel_id=1, source_target_pairs={{0,4},{4,8},{8,12},{12,0},{1,5},{5,9},{9,13},{13,1},{2,6},{6,10},{... | collective-permute-start | bytes 1572872 | tf_op jit(solution)/shard_map/ppermute | solution.py:24
  90.3 2.2 %collective-permute-start.3 = (f32[1,128,4,2,128]{4,2,3,1,0:T(4,128)S(1)}, f32[1,128,4,2,128]{4,2,3,1,0:T(4,128)S(1)}, u32[]{:S(2)}, u32[]{:S(2)}) collective-permute-start(f32[1,128,4,2,128]{4,2,3,1,0:T(4,128)S(1)} %bitcast.67), channel_id=1, source_target_pairs={{0,12},{4,0},{8,4},{12,8},{1,13},{5,1},{9,5},{13,9},{2,14},{6,2},{... | collective-permute-start | bytes 1572872 | tf_op jit(solution)/shard_map/ppermute | solution.py:27
  92.5 12.9 %collective-permute-done.2 = f32[1,128,4,2,128]{4,2,3,1,0:T(4,128)S(1)} collective-permute-done((f32[1,128,4,2,128]{4,2,3,1,0:T(4,128)S(1)}, f32[1,128,4,2,128]{4,2,3,1,0:T(4,128)S(1)}, u32[]{:S(2)}, u32[]{:S(2)}) %collective-permute-start.2) | collective-permute-done | bytes 524320 | tf_op jit(solution)/shard_map/ppermute | solution.py:24
  105.4 0.1 constant_dynamic-slice_fusion
  105.5 0.6 fusion.81
  109.9 0.3 broadcast_in_dim.47
  110.2 0.1 constant_dynamic-update-slice_fusion.3
  110.2 0.1 constant_dynamic-update-slice_fusion.2
  110.3 5.4 %collective-permute-done.3 = f32[1,128,4,2,128]{4,2,3,1,0:T(4,128)S(1)} collective-permute-done((f32[1,128,4,2,128]{4,2,3,1,0:T(4,128)S(1)}, f32[1,128,4,2,128]{4,2,3,1,0:T(4,128)S(1)}, u32[]{:S(2)}, u32[]{:S(2)}) %collective-permute-start.3) | collective-permute-done | bytes 524320 | tf_op jit(solution)/shard_map/ppermute | solution.py:27
  115.8 0.1 constant_dynamic-update-slice_fusion.1
  115.8 10.1 %collective-permute-done.4 = f32[1,128,4,2,128]{4,2,3,1,0:T(4,128)S(1)} collective-permute-done((f32[1,128,4,2,128]{4,2,3,1,0:T(4,128)S(1)}, f32[1,128,4,2,128]{4,2,3,1,0:T(4,128)S(1)}, u32[]{:S(2)}, u32[]{:S(2)}) %collective-permute-start.4) | collective-permute-done | bytes 524320 | tf_op jit(solution)/shard_map/ppermute | solution.py:24
  126.0 0.1 constant_dynamic-update-slice_fusion
  126.0 0.1 fusion.84
  126.2 0.1 select_select_fusion.2
  126.3 0.1 fusion.80
  126.5 0.1 maximum_bitcast_fusion.1
  126.6 31.0 %fusion.1 = bf16[1,1,128,2,128,128]{5,4,3,2,1,0:T(8,128)(2,1)} fusion(f32[4,128,4,2,128]{4,2,3,1,0:T(4,128)S(1)} %constant_dynamic-update-slice_fusion, s32[]{:T(128)} %bitcast.25, pred[]{:T(512)} %bitcast.24, pred[]{:T(512)} %bitcast.22, f32[1,128,1,4,2,128]{5,3,4,1,2,0:T(4,128)S(1)} %maximum_bitcast_fusion.1, f32[1,128,1,4,2,128]{5,3,4,1,2,0:T(4,128)S(1)} %fusion.84), kind=kOutput, calls=%fused_computation.3 | convolution fusion | flops 411566080 | bytes 9961478 | tf_op jit(solution)/shard_map/vmap(fpwqa,fwqb->fpab)/dot_general | solution.py:69
  (13 shorter events, 0.1 us)
Async XLA Ops:
  6.5 98.9 %copy-start = (s32[4,2]{0,1:T(2,128)S(1)}, s32[4,2]{0,1:T(2,128)}, u32[]{:S(2)}) copy-start(s32[4,2]{0,1:T(2,128)} %param.7) | copy-start | bytes 100
  6.5 18.0 %all-gather.2.cloned.1.call-start = ((), (), s32[]{:S(2)}) async-start(), calls=%async_computation.1 | async-start | bytes 5529600 | tf_op jit(solution)/shard_map/all_gather | solution.py:76
  24.6 25.0 %copy-start.1 = (f32[128,2,3600]{0,2,1:T(8,128)S(1)}, f32[128,2,3600]{0,2,1:T(8,128)}, u32[]{:S(2)}) copy-start(f32[128,2,3600]{0,2,1:T(8,128)} %all-gather.2.cloned.1.call-done) | copy-start | bytes 11059204
  71.1 3.5 %collective-permute-start = (f32[10,2,128]{2,0,1:T(8,128)S(1)}, f32[10,2,128]{2,0,1:T(8,128)S(1)}, u32[]{:S(2)}, u32[]{:S(2)}) collective-permute-start(f32[10,2,128]{2,0,1:T(8,128)S(1)} %get-tuple-element.19), channel_id=1, source_target_pairs={{0,1},{2,3},{4,5},{6,7},{8,9},{10,11},{12,13},{14,15},{16,17},{18,... | collective-permute-start | bytes 30728 | tf_op jit(solution)/shard_map/ppermute | solution.py:41
  73.2 3.1 %collective-permute-start.1 = (f32[10,2,128]{2,0,1:T(8,128)S(1)}, f32[10,2,128]{2,0,1:T(8,128)S(1)}, u32[]{:S(2)}, u32[]{:S(2)}) collective-permute-start(f32[10,2,128]{2,0,1:T(8,128)S(1)} %get-tuple-element.20), channel_id=1, source_target_pairs={{1,0},{3,2},{5,4},{7,6},{9,8},{11,10},{13,12},{15,14},{17,16},{19,... | collective-permute-start | bytes 30728 | tf_op jit(solution)/shard_map/ppermute | solution.py:42
  88.6 16.8 %collective-permute-start.2 = (f32[1,128,4,2,128]{4,2,3,1,0:T(4,128)S(1)}, f32[1,128,4,2,128]{4,2,3,1,0:T(4,128)S(1)}, u32[]{:S(2)}, u32[]{:S(2)}) collective-permute-start(f32[1,128,4,2,128]{4,2,3,1,0:T(4,128)S(1)} %bitcast.66), channel_id=1, source_target_pairs={{0,4},{4,8},{8,12},{12,0},{1,5},{5,9},{9,13},{13,1},{2,6},{6,10},{... | collective-permute-start | bytes 1572872 | tf_op jit(solution)/shard_map/ppermute | solution.py:24
  90.3 25.4 %collective-permute-start.3 = (f32[1,128,4,2,128]{4,2,3,1,0:T(4,128)S(1)}, f32[1,128,4,2,128]{4,2,3,1,0:T(4,128)S(1)}, u32[]{:S(2)}, u32[]{:S(2)}) collective-permute-start(f32[1,128,4,2,128]{4,2,3,1,0:T(4,128)S(1)} %bitcast.67), channel_id=1, source_target_pairs={{0,12},{4,0},{8,4},{12,8},{1,13},{5,1},{9,5},{13,9},{2,14},{6,2},{... | collective-permute-start | bytes 1572872 | tf_op jit(solution)/shard_map/ppermute | solution.py:27
  105.4 20.6 %collective-permute-start.4 = (f32[1,128,4,2,128]{4,2,3,1,0:T(4,128)S(1)}, f32[1,128,4,2,128]{4,2,3,1,0:T(4,128)S(1)}, u32[]{:S(2)}, u32[]{:S(2)}) collective-permute-start(f32[1,128,4,2,128]{4,2,3,1,0:T(4,128)S(1)} %collective-permute-done.2), channel_id=1, source_target_pairs={{0,4},{4,8},{8,12},{12,0},{1,5},{5,9},{9,13},{13,1},{2,6},{6,10},{... | collective-permute-start | bytes 1572872 | tf_op jit(solution)/shard_map/ppermute | solution.py:24
Sparse Core Ops, SparseCore 0:
  8.9 15.6 all-gather.1
